TPU v7x, 128 devices: a whole 4x4x4 slice. The times are simulated.
128 devices in a mesh: ax: 16 (over x, z), rad: 8 (over y, core).
Axes of the slice: x: 4, y: 4, z: 4, core: 2. Of those that a mesh axis runs over, the one named last changes fastest.
Arguments:
- forcing: float32 [32, 5, 256, 1024], P(None, None, 'ax', 'rad'), may hold values from -300 to 300, as said below
- vel_axial: float32 [256, 1024], P('ax', 'rad'), may hold values from 0.2 to 1
- vel_radial: float32 [256, 1024], P('ax', 'rad'), may hold values from -0.4 to 0.4
- coupling: float32 [5, 5, 256, 1024], P(None, None, 'ax', 'rad'), may hold values from -1.5 to 1.5
- viscosity: float32 [5], replicated, may hold values from 0.03 to 0.18
Outputs:
- basis: float32 [32, 5, 256, 1024], P(None, None, 'ax', 'rad')
- r_factor: float32 [32, 32], replicated
Inputs may be any that keep to these rules, and one draw needn't show every extreme that they name: `forcing`: forcing of the linearized equations.
All inputs are finite; a program needn't handle non-finite values.
Results may differ from a plain program's by a relative error of at most 0.00024.
Values sent between devices are 32-bit elements; how exact they have to be, the bound alone decides.
No kernel may reach another device: no remote copies, remote signals or barrier semaphores. Data moves between devices by JAX's collectives and lax.ppermute only.
A program may use at most 64 MiB of HBM per device.

v0:
```python
import jax
import jax.numpy as jnp
from jax import lax
from jax.sharding import PartitionSpec as P

STEPS = 3
time_step = 0.8


def padded_2(shard, sides, width):
    for axis, dim in sides:
        size, length = (lax.axis_size(axis), shard.shape[dim])
        up = [(i, (i + 1) % size) for i in range(size - 1)]
        down = [(j, i) for i, j in up]
        last = lax.slice_in_dim(shard, length - width, length, axis=dim)
        initial = lax.slice_in_dim(shard, 0, width, axis=dim)
        before = lax.ppermute(last, axis, up)
        after = lax.ppermute(initial, axis, down)
        shard = jnp.concatenate([before, shard, after], axis=dim)
    return shard


def combined_all(shard, axis, combine):
    everything = lax.all_gather(shard, axis)
    initial = everything[0]

    def turn(k, so_far):
        return combine(so_far, everything[k])

    return lax.fori_loop(1, lax.axis_size(axis), turn, initial)


def operate(padded, vel_axial, vel_radial, coupling, viscosity):
    center = padded[..., 2:-2, 2:-2]
    axial_up = padded[..., 3:-1, 2:-2]
    axial_down = padded[..., 1:-3, 2:-2]
    axial_far_up = padded[..., 4:, 2:-2]
    axial_far_down = padded[..., :-4, 2:-2]
    radial_up = padded[..., 2:-2, 3:-1]
    radial_down = padded[..., 2:-2, 1:-3]
    radial_far_up = padded[..., 2:-2, 4:]
    radial_far_down = padded[..., 2:-2, :-4]
    first_axial = (8.0 * (axial_up - axial_down) - (axial_far_up - axial_far_down)) / 12.0
    first_radial = (8.0 * (radial_up - radial_down) - (radial_far_up - radial_far_down)) / 12.0
    second = (
        16.0 * (axial_up + axial_down + radial_up + radial_down)
        - (axial_far_up + axial_far_down + radial_far_up + radial_far_down)
        - 60.0 * center
    ) / 12.0
    result = (
        -vel_axial * first_axial - vel_radial * first_radial + viscosity[:, None, None] * second
    )
    for source in range(coupling.shape[1]):
        result = result + coupling[:, source] * center[..., source : source + 1, :, :]
    return result


def upper_inverse(upper_factor):
    order = upper_factor.shape[0]
    identity = jnp.eye(order, dtype=jnp.float32)

    def one_row(count, inverse):
        row_index = order - 1 - count
        factor_row = lax.dynamic_slice_in_dim(upper_factor, row_index, 1, 0)
        unit_row = lax.dynamic_slice_in_dim(identity, row_index, 1, 0)
        pivot = jnp.sum(factor_row * unit_row)
        new_row = (unit_row - jnp.dot(factor_row, inverse, precision=lax.Precision.HIGHEST)) / pivot
        return lax.dynamic_update_slice_in_dim(inverse, new_row, row_index, 0)

    return lax.fori_loop(0, order, one_row, jnp.zeros((order, order), jnp.float32))


def rim_operator(field_now, vel_axial, vel_radial, coupling, viscosity):
    padded = padded_2(field_now, (("ax", 2), ("rad", 3)), 2)
    return operate(padded, vel_axial, vel_radial, coupling, viscosity)


def join_factors(first_factor, other_factor):
    summed = jnp.dot(first_factor.T, first_factor, precision=lax.Precision.HIGHEST)
    summed = summed + jnp.dot(other_factor.T, other_factor, precision=lax.Precision.HIGHEST)
    return jnp.linalg.cholesky(summed).T


def per_device(forcing, vel_axial, vel_radial, coupling, viscosity):
    vectors, variables, axial_cells, radial_cells = forcing.shape
    field_now = forcing
    for step_index in range(STEPS):
        slope_one = rim_operator(field_now, vel_axial, vel_radial, coupling, viscosity)
        middle = field_now + time_step * slope_one
        slope_two = rim_operator(middle, vel_axial, vel_radial, coupling, viscosity)
        field_now = field_now + 0.5 * time_step * (slope_one + slope_two)
    flattened = field_now.reshape(vectors, variables * axial_cells * radial_cells)
    rows_all = variables * axial_cells * radial_cells * lax.axis_size("ax") * lax.axis_size("rad")
    local_gram = jnp.dot(flattened, flattened.T, precision=lax.Precision.HIGHEST) / rows_all
    radial_gram = lax.psum(local_gram, "rad")
    start_factor = jnp.linalg.cholesky(radial_gram).T
    upper_factor = combined_all(start_factor, "ax", join_factors)
    inverse = upper_inverse(upper_factor)
    basis = jnp.dot(inverse.T, flattened, precision=lax.Precision.HIGHEST).reshape(field_now.shape)
    return (basis, upper_factor)


def solution(mesh):
    return jax.shard_map(
        per_device,
        mesh=mesh,
        in_specs=(
            P(None, None, "ax", "rad"),
            P("ax", "rad"),
            P("ax", "rad"),
            P(None, None, "ax", "rad"),
            P(),
        ),
        out_specs=(P(None, None, "ax", "rad"), P()),
        check_vma=False,
    )
```

profile of v0, /device:TPU:0, one launch (start us, length us, event | category | flops | bytes accessed | tf_op | source)
XLA Modules:
  0.0 470.0 jit_solution(13325855620133303022)
XLA Ops:
  2.8 4.6 collective-permute-start.1
  9.4 4.3 copy.227
  19.7 3.5 pad_maximum_fusion
  23.2 3.1 copy-done.1
  27.6 3.0 collective-permute-start.3
  35.9 6.5 %copy.229 = f32[32,5,20,128]{3,0,2,1:T(8,128)} copy(f32[32,5,20,128]{0,2,3,1:T(8,128)} %copy-done.1) | data formatting | bytes 3276800 | tf_op jit(solution)/shard_map/concatenate | solution.py:19
  46.1 8.8 %multiply_add_fusion.7 = (f32[32,5,16,128]{3,0,2,1:T(8,128)S(1)}, f32[32,5,16,128]{3,0,2,1:T(8,128)}) fusion(f32[32,5,16,128]{3,2,1,0:T(8,128)S(1)} %copy-done, f32[32,16,128]{2,0,1:T(8,128)} %copy.238, f32[5,16,128]{2,1,0:T(8,128)S(1)} %get-tuple-element.336, f32[32,16,128]{2,0,1:T(8,128)} %copy.237, f32[5,16,128]{2,1,0:T(8,128)S(1)} %get-tuple-element.337, ...), kind=kLoop, calls=%fused_computation.117 | loop fusion | flops 12779520 | bytes 12396564 | tf_op jit(solution)/shard_map/add | solution.py:89
  56.3 5.2 %collective-permute-start.5 = (f32[32,5,2,128]{3,0,2,1:T(8,128)S(1)}, f32[32,5,2,128]{3,0,2,1:T(8,128)S(1)}, u32[]{:S(2)}, u32[]{:S(2)}) collective-permute-start(f32[32,5,2,128]{3,0,2,1:T(8,128)S(1)} %get-tuple-element.322), channel_id=1, source_target_pairs={{0,8},{8,16},{16,24},{24,32},{32,40},{40,48},{48,56},{56,64},{64,7... | collective-permute-start | bytes 491528 | tf_op jit(solution)/shard_map/ppermute | solution.py:17
  61.5 2.7 collective-permute-done.4
  66.5 2.2 fusion.27
  68.7 2.2 copy.277
  72.2 2.9 copy.278
  75.1 3.7 collective-permute-start.7
  79.7 2.8 copy.241
  82.5 2.7 copy.243
  85.2 9.3 %multiply_add_fusion.6 = f32[32,5,16,128]{3,0,2,1:T(8,128)S(1)} fusion(f32[32,5,16,128]{3,0,2,1:T(8,128)} %get-tuple-element.276, f32[32,5,16,128]{3,0,2,1:T(8,128)} %copy-done.2, f32[32,5,20,2]{3,0,2,1:T(8,128)} %copy.241, f32[32,5,2,128]{3,0,2,1:T(8,128)} %copy-done.7, f32[32,5,2,128]{3,0,2,1:T(8,128)} %copy-done.11, f32[32,5,20,2]{3,0,2,1:T(8,128)} %copy.243, ...), kind=kLoop, calls=%fused_computation.116 | loop fusion | flops 17039360 | bytes 7153684 | tf_op jit(solution)/shard_map/add | solution.py:91
  95.8 5.2 %collective-permute-start.9 = (f32[32,5,2,128]{3,0,2,1:T(8,128)S(1)}, f32[32,5,2,128]{3,0,2,1:T(8,128)S(1)}, u32[]{:S(2)}, u32[]{:S(2)}) collective-permute-start(f32[32,5,2,128]{3,0,2,1:T(8,128)S(1)} %get-tuple-element.310), channel_id=1, source_target_pairs={{0,8},{8,16},{16,24},{24,32},{32,40},{40,48},{48,56},{56,64},{64,7... | collective-permute-start | bytes 491528 | tf_op jit(solution)/shard_map/ppermute | solution.py:17
  101.0 2.9 collective-permute-done.8
  105.8 2.3 fusion.26
  108.2 2.2 copy.279
  111.7 2.2 copy.280
  113.9 3.0 collective-permute-start.11
  121.5 5.9 %multiply_add_fusion.4 = (f32[32,5,16,128]{3,0,2,1:T(8,128)S(1)}, f32[32,5,16,128]{3,0,2,1:T(8,128)}) fusion(f32[32,5,16,128]{3,0,2,1:T(8,128)S(1)} %multiply_add_fusion.6, f32[32,16,128]{2,0,1:T(8,128)} %get-tuple-element.316, f32[5,16,128]{2,1,0:T(8,128)S(1)} %get-tuple-element.336, f32[32,16,128]{2,0,1:T(8,128)S(1)} %get-tuple-element.313, ...), kind=kLoop, calls=%fused_computation.114 | loop fusion | flops 16711680 | bytes 5842964 | tf_op jit(solution)/shard_map/add | solution.py:89
  128.7 5.0 %collective-permute-start.13 = (f32[32,5,2,128]{3,0,2,1:T(8,128)S(1)}, f32[32,5,2,128]{3,0,2,1:T(8,128)S(1)}, u32[]{:S(2)}, u32[]{:S(2)}) collective-permute-start(f32[32,5,2,128]{3,0,2,1:T(8,128)S(1)} %get-tuple-element.308), channel_id=1, source_target_pairs={{0,8},{8,16},{16,24},{24,32},{32,40},{40,48},{48,56},{56,64},{64,7... | collective-permute-start | bytes 491528 | tf_op jit(solution)/shard_map/ppermute | solution.py:17
  133.8 2.7 collective-permute-done.12
  138.8 2.2 fusion.25
  144.5 2.9 copy.282
  147.4 3.7 collective-permute-start.15
  152.0 2.8 copy.250
  154.8 2.7 copy.252
  157.5 9.2 %multiply_add_fusion.3 = f32[32,5,16,128]{3,0,2,1:T(8,128)S(1)} fusion(f32[32,5,16,128]{3,0,2,1:T(8,128)S(1)} %multiply_add_fusion.6, f32[32,5,16,128]{3,0,2,1:T(8,128)} %get-tuple-element.274, f32[32,5,16,128]{3,0,2,1:T(8,128)} %copy-done.3, f32[32,5,20,2]{3,0,2,1:T(8,128)} %copy.250, f32[32,5,2,128]{3,0,2,1:T(8,128)} %copy-done.6, ...), kind=kLoop, calls=%fused_computation.113 | loop fusion | flops 17039360 | bytes 7153684 | tf_op jit(solution)/shard_map/add | solution.py:91
  168.1 5.0 %collective-permute-start.17 = (f32[32,5,2,128]{3,0,2,1:T(8,128)S(1)}, f32[32,5,2,128]{3,0,2,1:T(8,128)S(1)}, u32[]{:S(2)}, u32[]{:S(2)}) collective-permute-start(f32[32,5,2,128]{3,0,2,1:T(8,128)S(1)} %get-tuple-element.296), channel_id=1, source_target_pairs={{0,8},{8,16},{16,24},{24,32},{32,40},{40,48},{48,56},{56,64},{64,7... | collective-permute-start | bytes 491528 | tf_op jit(solution)/shard_map/ppermute | solution.py:17
  173.1 2.8 collective-permute-done.16
  180.2 2.2 copy.283
  185.1 3.2 collective-permute-start.19
  189.3 2.8 copy.254
  193.9 5.9 %multiply_add_fusion.1 = (f32[32,5,16,128]{3,0,2,1:T(8,128)S(1)}, f32[32,5,16,128]{3,0,2,1:T(8,128)}) fusion(f32[32,5,16,128]{3,0,2,1:T(8,128)S(1)} %multiply_add_fusion.3, f32[32,16,128]{2,0,1:T(8,128)} %get-tuple-element.302, f32[5,16,128]{2,1,0:T(8,128)S(1)} %get-tuple-element.336, f32[32,16,128]{2,0,1:T(8,128)S(1)} %get-tuple-element.299, ...), kind=kLoop, calls=%fused_computation.111 | loop fusion | flops 16711680 | bytes 5842964 | tf_op jit(solution)/shard_map/add | solution.py:89
  201.7 6.8 %collective-permute-start.21 = (f32[32,5,2,128]{3,0,2,1:T(8,128)S(1)}, f32[32,5,2,128]{3,0,2,1:T(8,128)S(1)}, u32[]{:S(2)}, u32[]{:S(2)}) collective-permute-start(f32[32,5,2,128]{3,0,2,1:T(8,128)S(1)} %get-tuple-element.294), channel_id=1, source_target_pairs={{0,8},{8,16},{16,24},{24,32},{32,40},{40,48},{48,56},{56,64},{64,7... | collective-permute-start | bytes 491528 | tf_op jit(solution)/shard_map/ppermute | solution.py:17
  213.4 2.2 fusion.23
  219.2 2.9 copy.286
  222.0 3.7 collective-permute-start.23
  226.6 2.8 copy.258
  229.4 2.7 copy.260
  232.1 5.3 %multiply_add_fusion = f32[32,5,16,128]{3,0,2,1:T(8,128)S(1)} fusion(f32[32,5,16,128]{3,0,2,1:T(8,128)S(1)} %multiply_add_fusion.3, f32[32,5,16,128]{3,0,2,1:T(8,128)} %get-tuple-element.272, f32[32,5,16,128]{3,0,2,1:T(8,128)S(1)} %get-tuple-element.271, f32[32,5,20,2]{3,0,2,1:T(8,128)} %copy.258, f32[32,5,2,128]{3,0,2,1:T(8,128)} %copy-done.4, ...), kind=kLoop, calls=%fused_computation.110 | loop fusion | flops 17039360 | bytes 7153684 | tf_op jit(solution)/shard_map/add | solution.py:91
  239.3 24.5 %psum.7 = f32[32,32]{0,1:T(8,128)S(1)} all-reduce(f32[32,32]{0,1:T(8,128)S(1)} %fusion.18), channel_id=1, replica_groups=mesh['ax'=16,'rad'=8] {'rad'}, use_global_device_ids=true, to_apply=%region_0.0 | all-reduce | flops 1024 | bytes 8192 | tf_op jit(solution)/shard_map/psum | solution.py:95
  264.0 2.9 cholesky.55
  268.3 36.5 %all-gather = f32[512,32]{1,0:T(8,128)S(1)} all-gather(f32[32,32]{1,0:T(8,128)S(1)} %copy.263), channel_id=2, replica_groups=mesh['ax'=16,'rad'=8] {'ax'}, dimensions={0}, use_global_device_ids=true | all-gather | bytes 69632 | tf_op jit(solution)/shard_map/all_gather | solution.py:24
  304.8 70.9 %while.30 = (s32[]{:T(128)}, f32[32,32]{0,1:T(8,128)S(1)}, f32[16,32,32]{2,1,0:T(8,128)S(1)}, s32[]{:T(128)}, s32[]{:T(128)}, /*index=5*/s32[]{:T(128)}) while((s32[]{:T(128)}, f32[32,32]{0,1:T(8,128)S(1)}, f32[16,32,32]{2,1,0:T(8,128)S(1)}, s32[]{:T(128)}, s32[]{:T(128)}, /*index=5*/s32[]{:T(128)}) %tuple.141), condition=%wide.region_4.6_spmd, body=%wide.region_3.5_spmd.sunk | while | flops 795684 | bytes 78197 | solution.py:30
  305.3 2.9 cholesky.109
  310.0 2.9 cholesky.109
  314.8 2.9 cholesky.109
  319.5 2.9 cholesky.109
  324.2 2.9 cholesky.109
  329.0 2.9 cholesky.109
  333.7 2.9 cholesky.109
  338.4 2.9 cholesky.109
  343.1 2.9 cholesky.109
  347.9 2.9 cholesky.109
  352.6 2.9 cholesky.109
  357.3 2.9 cholesky.109
  362.1 2.9 cholesky.109
  366.8 2.9 cholesky.109
  371.5 2.9 cholesky.109
  375.9 90.0 %while.31 = (s32[]{:T(128)}, f32[32,32]{1,0:T(8,128)S(1)}, f32[32,32]{1,0:T(8,128)}, f32[32,32]{1,0:T(8,128)S(1)}, s32[]{:T(128)}, /*index=5*/s32[]{:T(128)}, s32[]{:T(128)}, s32[]{:T(128)}) while((s32[]{:T(128)}, f32[32,32]{1,0:T(8,128)S(1)}, f32[32,32]{1,0:T(8,128)}, f32[32,32]{1,0:T(8,128)S(1)}, s32[]{:T(128)}, /*index=5*/s32[]{:T(128)}, ...), condition=%wide.region_7.9_spmd, body=%wide.region_5.8_spmd.sunk | while | flops 12421 | bytes 18835 | solution.py:70
  (339 shorter events, 189.1 us)
Async XLA Ops:
  0.6 8.7 %copy-start = (f32[32,5,16,128]{3,2,1,0:T(8,128)S(1)}, f32[32,5,16,128]{3,2,1,0:T(8,128)}, u32[]{:S(2)}) copy-start(f32[32,5,16,128]{3,2,1,0:T(8,128)} %param.10) | copy-start | bytes 3932164
  2.8 14.4 %collective-permute-start.1 = (f32[32,5,2,128]{3,0,2,1:T(8,128)}, f32[32,5,2,128]{3,0,2,1:T(8,128)}, u32[]{:S(2)}, u32[]{:S(2)}) collective-permute-start(f32[32,5,2,128]{3,0,2,1:T(8,128)} %copy.298), channel_id=1, source_target_pairs={{0,8},{8,16},{16,24},{24,32},{32,40},{40,48},{48,56},{56,64},{64,7... | collective-permute-start | bytes 491528 | tf_op jit(solution)/shard_map/ppermute | solution.py:17
  8.1 10.4 %collective-permute-start = (f32[32,5,2,128]{3,0,2,1:T(8,128)}, f32[32,5,2,128]{3,0,2,1:T(8,128)}, u32[]{:S(2)}, u32[]{:S(2)}) collective-permute-start(f32[32,5,2,128]{3,0,2,1:T(8,128)} %copy.297), channel_id=1, source_target_pairs={{8,0},{16,8},{24,16},{32,24},{40,32},{48,40},{56,48},{64,56},{72,6... | collective-permute-start | bytes 491528 | tf_op jit(solution)/shard_map/ppermute | solution.py:18
  13.7 0.9 copy-start.14
  14.6 2.6 copy-start.21
  14.6 2.6 copy-start.22
  14.6 2.6 copy-start.23
  17.2 28.9 %copy-start.16 = (f32[5]{0:T(128)}, f32[5]{0:T(128)S(1)}, u32[]{:S(2)}) copy-start(f32[5]{0:T(128)S(1)} %broadcast_multiply_fusion.1) | copy-start | bytes 64
  23.2 3.1 copy-start.1
  26.3 16.1 %collective-permute-start.2 = (f32[32,5,20,2]{0,2,3,1:T(8,128)S(1)}, f32[32,5,20,2]{0,2,3,1:T(8,128)S(1)}, u32[]{:S(2)}, u32[]{:S(2)}) collective-permute-start(f32[32,5,20,2]{0,2,3,1:T(8,128)S(1)} %get-tuple-element.277), channel_id=1, source_target_pairs={{1,0},{2,1},{3,2},{4,3},{5,4},{6,5},{7,6},{9,8},{10,9},{11,10},{12... | collective-permute-start | bytes 76808 | tf_op jit(solution)/shard_map/ppermute | solution.py:18
  27.6 16.7 %collective-permute-start.3 = (f32[32,5,20,2]{0,2,3,1:T(8,128)S(1)}, f32[32,5,20,2]{0,2,3,1:T(8,128)S(1)}, u32[]{:S(2)}, u32[]{:S(2)}) collective-permute-start(f32[32,5,20,2]{0,2,3,1:T(8,128)S(1)} %get-tuple-element.278), channel_id=1, source_target_pairs={{0,1},{1,2},{2,3},{3,4},{4,5},{5,6},{6,7},{8,9},{9,10},{10,11},{11... | collective-permute-start | bytes 76808 | tf_op jit(solution)/shard_map/ppermute | solution.py:17
  54.9 23.8 %copy-start.2 = (f32[32,5,16,128]{3,0,2,1:T(8,128)}, f32[32,5,16,128]{3,0,2,1:T(8,128)S(1)}, u32[]{:S(2)}) copy-start(f32[32,5,16,128]{3,0,2,1:T(8,128)S(1)} %get-tuple-element.275) | copy-start | bytes 3932164
  55.0 9.2 %collective-permute-start.4 = (f32[32,5,2,128]{3,0,2,1:T(8,128)S(1)}, f32[32,5,2,128]{3,0,2,1:T(8,128)S(1)}, u32[]{:S(2)}, u32[]{:S(2)}) collective-permute-start(f32[32,5,2,128]{3,0,2,1:T(8,128)S(1)} %get-tuple-element.323), channel_id=1, source_target_pairs={{8,0},{16,8},{24,16},{32,24},{40,32},{48,40},{56,48},{64,56},{72,6... | collective-permute-start | bytes 491528 | tf_op jit(solution)/shard_map/ppermute | solution.py:18
  56.3 9.5 %collective-permute-start.5 = (f32[32,5,2,128]{3,0,2,1:T(8,128)S(1)}, f32[32,5,2,128]{3,0,2,1:T(8,128)S(1)}, u32[]{:S(2)}, u32[]{:S(2)}) collective-permute-start(f32[32,5,2,128]{3,0,2,1:T(8,128)S(1)} %get-tuple-element.322), channel_id=1, source_target_pairs={{0,8},{8,16},{16,24},{24,32},{32,40},{40,48},{48,56},{56,64},{64,7... | collective-permute-start | bytes 491528 | tf_op jit(solution)/shard_map/ppermute | solution.py:17
  64.1 1.8 copy-start.7
  65.8 0.7 copy-start.11
  70.9 8.8 %collective-permute-start.6 = (f32[32,5,20,2]{0,2,3,1:T(8,128)S(1)}, f32[32,5,20,2]{0,2,3,1:T(8,128)}, u32[]{:S(2)}, u32[]{:S(2)}) collective-permute-start(f32[32,5,20,2]{0,2,3,1:T(8,128)S(1)} %copy.277), channel_id=1, source_target_pairs={{1,0},{2,1},{3,2},{4,3},{5,4},{6,5},{7,6},{9,8},{10,9},{11,10},{12... | collective-permute-start | bytes 76808 | tf_op jit(solution)/shard_map/ppermute | solution.py:18
  75.1 7.4 %collective-permute-start.7 = (f32[32,5,20,2]{0,2,3,1:T(8,128)}, f32[32,5,20,2]{0,2,3,1:T(8,128)}, u32[]{:S(2)}, u32[]{:S(2)}) collective-permute-start(f32[32,5,20,2]{0,2,3,1:T(8,128)} %copy.278), channel_id=1, source_target_pairs={{0,1},{1,2},{2,3},{3,4},{4,5},{5,6},{6,7},{8,9},{9,10},{10,11},{11... | collective-permute-start | bytes 76808 | tf_op jit(solution)/shard_map/ppermute | solution.py:17
  82.5 2.7 copy-start.17
  94.5 9.4 %collective-permute-start.8 = (f32[32,5,2,128]{3,0,2,1:T(8,128)S(1)}, f32[32,5,2,128]{3,0,2,1:T(8,128)S(1)}, u32[]{:S(2)}, u32[]{:S(2)}) collective-permute-start(f32[32,5,2,128]{3,0,2,1:T(8,128)S(1)} %get-tuple-element.311), channel_id=1, source_target_pairs={{8,0},{16,8},{24,16},{32,24},{40,32},{48,40},{56,48},{64,56},{72,6... | collective-permute-start | bytes 491528 | tf_op jit(solution)/shard_map/ppermute | solution.py:18
  95.8 9.3 %collective-permute-start.9 = (f32[32,5,2,128]{3,0,2,1:T(8,128)S(1)}, f32[32,5,2,128]{3,0,2,1:T(8,128)S(1)}, u32[]{:S(2)}, u32[]{:S(2)}) collective-permute-start(f32[32,5,2,128]{3,0,2,1:T(8,128)S(1)} %get-tuple-element.310), channel_id=1, source_target_pairs={{0,8},{8,16},{16,24},{24,32},{32,40},{40,48},{48,56},{56,64},{64,7... | collective-permute-start | bytes 491528 | tf_op jit(solution)/shard_map/ppermute | solution.py:17
  104.0 1.3 copy-start.8
  105.2 0.7 copy-start.12
  110.4 7.5 %collective-permute-start.10 = (f32[32,5,20,2]{0,2,3,1:T(8,128)S(1)}, f32[32,5,20,2]{0,2,3,1:T(8,128)S(1)}, u32[]{:S(2)}, u32[]{:S(2)}) collective-permute-start(f32[32,5,20,2]{0,2,3,1:T(8,128)S(1)} %copy.279), channel_id=1, source_target_pairs={{1,0},{2,1},{3,2},{4,3},{5,4},{6,5},{7,6},{9,8},{10,9},{11,10},{12... | collective-permute-start | bytes 76808 | tf_op jit(solution)/shard_map/ppermute | solution.py:18
  113.9 5.8 %collective-permute-start.11 = (f32[32,5,20,2]{0,2,3,1:T(8,128)S(1)}, f32[32,5,20,2]{0,2,3,1:T(8,128)S(1)}, u32[]{:S(2)}, u32[]{:S(2)}) collective-permute-start(f32[32,5,20,2]{0,2,3,1:T(8,128)S(1)} %copy.280), channel_id=1, source_target_pairs={{0,1},{1,2},{2,3},{3,4},{4,5},{5,6},{6,7},{8,9},{9,10},{10,11},{11... | collective-permute-start | bytes 76808 | tf_op jit(solution)/shard_map/ppermute | solution.py:17
  127.4 23.7 %copy-start.3 = (f32[32,5,16,128]{3,0,2,1:T(8,128)}, f32[32,5,16,128]{3,0,2,1:T(8,128)S(1)}, u32[]{:S(2)}) copy-start(f32[32,5,16,128]{3,0,2,1:T(8,128)S(1)} %get-tuple-element.273) | copy-start | bytes 3932164
  127.4 9.0 %collective-permute-start.12 = (f32[32,5,2,128]{3,0,2,1:T(8,128)S(1)}, f32[32,5,2,128]{3,0,2,1:T(8,128)S(1)}, u32[]{:S(2)}, u32[]{:S(2)}) collective-permute-start(f32[32,5,2,128]{3,0,2,1:T(8,128)S(1)} %get-tuple-element.309), channel_id=1, source_target_pairs={{8,0},{16,8},{24,16},{32,24},{40,32},{48,40},{56,48},{64,56},{72,6... | collective-permute-start | bytes 491528 | tf_op jit(solution)/shard_map/ppermute | solution.py:18
  128.7 9.4 %collective-permute-start.13 = (f32[32,5,2,128]{3,0,2,1:T(8,128)S(1)}, f32[32,5,2,128]{3,0,2,1:T(8,128)S(1)}, u32[]{:S(2)}, u32[]{:S(2)}) collective-permute-start(f32[32,5,2,128]{3,0,2,1:T(8,128)S(1)} %get-tuple-element.308), channel_id=1, source_target_pairs={{0,8},{8,16},{16,24},{24,32},{32,40},{40,48},{48,56},{56,64},{64,7... | collective-permute-start | bytes 491528 | tf_op jit(solution)/shard_map/ppermute | solution.py:17
  136.4 1.8 copy-start.6
  138.1 0.7 copy-start.10
  143.2 8.8 %collective-permute-start.14 = (f32[32,5,20,2]{0,2,3,1:T(8,128)S(1)}, f32[32,5,20,2]{0,2,3,1:T(8,128)}, u32[]{:S(2)}, u32[]{:S(2)}) collective-permute-start(f32[32,5,20,2]{0,2,3,1:T(8,128)S(1)} %copy.281), channel_id=1, source_target_pairs={{1,0},{2,1},{3,2},{4,3},{5,4},{6,5},{7,6},{9,8},{10,9},{11,10},{12... | collective-permute-start | bytes 76808 | tf_op jit(solution)/shard_map/ppermute | solution.py:18
  147.4 7.4 %collective-permute-start.15 = (f32[32,5,20,2]{0,2,3,1:T(8,128)}, f32[32,5,20,2]{0,2,3,1:T(8,128)}, u32[]{:S(2)}, u32[]{:S(2)}) collective-permute-start(f32[32,5,20,2]{0,2,3,1:T(8,128)} %copy.282), channel_id=1, source_target_pairs={{0,1},{1,2},{2,3},{3,4},{4,5},{5,6},{6,7},{8,9},{9,10},{10,11},{11... | collective-permute-start | bytes 76808 | tf_op jit(solution)/shard_map/ppermute | solution.py:17
  154.8 2.7 copy-start.18
  166.8 9.1 %collective-permute-start.16 = (f32[32,5,2,128]{3,0,2,1:T(8,128)S(1)}, f32[32,5,2,128]{3,0,2,1:T(8,128)S(1)}, u32[]{:S(2)}, u32[]{:S(2)}) collective-permute-start(f32[32,5,2,128]{3,0,2,1:T(8,128)S(1)} %get-tuple-element.297), channel_id=1, source_target_pairs={{8,0},{16,8},{24,16},{32,24},{40,32},{48,40},{56,48},{64,56},{72,6... | collective-permute-start | bytes 491528 | tf_op jit(solution)/shard_map/ppermute | solution.py:18
  168.1 9.5 %collective-permute-start.17 = (f32[32,5,2,128]{3,0,2,1:T(8,128)S(1)}, f32[32,5,2,128]{3,0,2,1:T(8,128)S(1)}, u32[]{:S(2)}, u32[]{:S(2)}) collective-permute-start(f32[32,5,2,128]{3,0,2,1:T(8,128)S(1)} %get-tuple-element.296), channel_id=1, source_target_pairs={{0,8},{8,16},{16,24},{24,32},{32,40},{40,48},{48,56},{56,64},{64,7... | collective-permute-start | bytes 491528 | tf_op jit(solution)/shard_map/ppermute | solution.py:17
  175.9 1.7 copy-start.9
  177.6 0.7 copy-start.13
  182.4 6.9 %collective-permute-start.18 = (f32[32,5,20,2]{0,2,3,1:T(8,128)S(1)}, f32[32,5,20,2]{0,2,3,1:T(8,128)}, u32[]{:S(2)}, u32[]{:S(2)}) collective-permute-start(f32[32,5,20,2]{0,2,3,1:T(8,128)S(1)} %copy.283), channel_id=1, source_target_pairs={{1,0},{2,1},{3,2},{4,3},{5,4},{6,5},{7,6},{9,8},{10,9},{11,10},{12... | collective-permute-start | bytes 76808 | tf_op jit(solution)/shard_map/ppermute | solution.py:18
  185.1 6.9 %collective-permute-start.19 = (f32[32,5,20,2]{0,2,3,1:T(8,128)}, f32[32,5,20,2]{0,2,3,1:T(8,128)S(1)}, u32[]{:S(2)}, u32[]{:S(2)}) collective-permute-start(f32[32,5,20,2]{0,2,3,1:T(8,128)} %copy.284), channel_id=1, source_target_pairs={{0,1},{1,2},{2,3},{3,4},{4,5},{5,6},{6,7},{8,9},{9,10},{10,11},{11... | collective-permute-start | bytes 76808 | tf_op jit(solution)/shard_map/ppermute | solution.py:17
  192.0 1.8 copy-start.19
  200.4 10.7 %collective-permute-start.20 = (f32[32,5,2,128]{3,0,2,1:T(8,128)}, f32[32,5,2,128]{3,0,2,1:T(8,128)S(1)}, u32[]{:S(2)}, u32[]{:S(2)}) collective-permute-start(f32[32,5,2,128]{3,0,2,1:T(8,128)} %get-tuple-element.295), channel_id=1, source_target_pairs={{8,0},{16,8},{24,16},{32,24},{40,32},{48,40},{56,48},{64,56},{72,6... | collective-permute-start | bytes 491528 | tf_op jit(solution)/shard_map/ppermute | solution.py:18
  201.7 11.0 %collective-permute-start.21 = (f32[32,5,2,128]{3,0,2,1:T(8,128)S(1)}, f32[32,5,2,128]{3,0,2,1:T(8,128)S(1)}, u32[]{:S(2)}, u32[]{:S(2)}) collective-permute-start(f32[32,5,2,128]{3,0,2,1:T(8,128)S(1)} %get-tuple-element.294), channel_id=1, source_target_pairs={{0,8},{8,16},{16,24},{24,32},{32,40},{40,48},{48,56},{56,64},{64,7... | collective-permute-start | bytes 491528 | tf_op jit(solution)/shard_map/ppermute | solution.py:17
  211.2 1.7 copy-start.4
  212.7 0.7 copy-start.5
  217.9 8.7 %collective-permute-start.22 = (f32[32,5,20,2]{0,2,3,1:T(8,128)S(1)}, f32[32,5,20,2]{0,2,3,1:T(8,128)}, u32[]{:S(2)}, u32[]{:S(2)}) collective-permute-start(f32[32,5,20,2]{0,2,3,1:T(8,128)S(1)} %copy.285), channel_id=1, source_target_pairs={{1,0},{2,1},{3,2},{4,3},{5,4},{6,5},{7,6},{9,8},{10,9},{11,10},{12... | collective-permute-start | bytes 76808 | tf_op jit(solution)/shard_map/ppermute | solution.py:18
  222.0 7.4 %collective-permute-start.23 = (f32[32,5,20,2]{0,2,3,1:T(8,128)}, f32[32,5,20,2]{0,2,3,1:T(8,128)}, u32[]{:S(2)}, u32[]{:S(2)}) collective-permute-start(f32[32,5,20,2]{0,2,3,1:T(8,128)} %copy.286), channel_id=1, source_target_pairs={{0,1},{1,2},{2,3},{3,4},{4,5},{5,6},{6,7},{8,9},{9,10},{10,11},{11... | collective-permute-start | bytes 76808 | tf_op jit(solution)/shard_map/ppermute | solution.py:17
  229.4 2.7 copy-start.20
  465.9 0.6 copy-start.15
where the time goes:
time: 474 us; the launch traced here: 470 us
  other arithmetic  159 us (34%)
  local copies, waits for them, and re-layouts  104 us (22%)
  starting transfers between devices  67.7 us (14%)
  blocking collectives  61 us (13%)
  matrix products  54.9 us (12%)
  waiting for transfers between devices  20.9 us (4%)
    another operation x45, other arithmetic, join_factors(): return jnp.linalg.cholesky(summed).T  53.9 us
    ppermute x12, starting transfers between devices, padded_2(): before = lax.ppermute(last, axis, up)  52.2 us
    dot_general x32, matrix products, one_row(): jnp.dot(factor_row, inverse, precision=lax.Precision.HIGHEST)  46.9 us
    unnamed x66, local copies, waits for them, and re-layouts  41.9 us
    reduce_sum x32, other arithmetic, one_row(): pivot = jnp.sum(factor_row * unit_row)  41.6 us
    all_gather x1, blocking collectives, combined_all(): everything = lax.all_gather(shard, axis)  36.5 us
    psum x1, blocking collectives, per_device(): radial_gram = lax.psum(local_gram, 'rad')  24.5 us
    add x3, other arithmetic, per_device(): field_now = field_now + 0.5 * time_step * (slope_one + slope_two)  23.8 us
  transfers between devices with their start and end apart: 24, of which 10 were waited for; matrix products, arithmetic and copies ran while one was open for 11% of the time, Pallas kernels for 0%

commit v1 on v0

--- a/solution.py
+++ b/solution.py
@@ -5,6 +5,15 @@
 
 STEPS = 3
 time_step = 0.8
+
+
+def doubling_sum(x, axis):
+    peers = lax.axis_size(axis)
+    total, far = (x, 1)
+    while far < peers:
+        total = total + lax.ppermute(total, axis, [(i, i ^ far) for i in range(peers)])
+        far = 2 * far
+    return total
 
 
 def padded_2(shard, sides, width):
@@ -92,7 +101,7 @@
     flattened = field_now.reshape(vectors, variables * axial_cells * radial_cells)
     rows_all = variables * axial_cells * radial_cells * lax.axis_size("ax") * lax.axis_size("rad")
     local_gram = jnp.dot(flattened, flattened.T, precision=lax.Precision.HIGHEST) / rows_all
-    radial_gram = lax.psum(local_gram, "rad")
+    radial_gram = doubling_sum(local_gram, "rad")
     start_factor = jnp.linalg.cholesky(radial_gram).T
     upper_factor = combined_all(start_factor, "ax", join_factors)
     inverse = upper_inverse(upper_factor)

time: 474 us -> 412 us (0.87)
  blocking collectives: 61 us -> 36.5 us
  other arithmetic: 159 us -> 136 us
  matrix products: 54.9 us -> 33 us
  waiting for transfers between devices: 20.9 us -> 26.9 us
    psum x1 -> x0, blocking collectives: 24.5 us -> none  [per_device(): radial_gram = lax.psum(local_gram, 'rad')]
    reduce_sum x32, other arithmetic: 41.6 us -> 19.5 us  [one_row(): pivot = jnp.sum(factor_row * unit_row)]
    dot_general x32, matrix products: 46.9 us -> 24.9 us  [one_row(): jnp.dot(factor_row, inverse, precision=lax.Precision.HIGHEST)]
    ppermute x0 -> x3, waiting for transfers between devices: none -> 5.42 us  [doubling_sum(): lax.ppermute(total, axis, [(i, i ^ far) for i in range(peers)])]
    unnamed x66 -> x68, local copies, waits for them, and re-layouts: 41.9 us -> 41.6 us
  transfers between devices with their start and end apart: 24 -> 27, of which waited for: 10 -> 13; matrix products, arithmetic and copies ran while one was open for 11% -> 13% of each run, Pallas kernels for 0% -> 0%
where the time goes in v1:
time: 412 us; the launch traced here: 410 us
  other arithmetic  136 us (33%)
  local copies, waits for them, and re-layouts  105 us (25%)
  starting transfers between devices  70.6 us (17%)
  blocking collectives  36.5 us (9%)
  matrix products  33 us (8%)
  waiting for transfers between devices  26.9 us (7%)
    another operation x45, other arithmetic, join_factors(): return jnp.linalg.cholesky(summed).T  53.9 us
    ppermute x12, starting transfers between devices, padded_2(): before = lax.ppermute(last, axis, up)  52.2 us
    unnamed x68, local copies, waits for them, and re-layouts  41.6 us
    all_gather x1, blocking collectives, combined_all(): everything = lax.all_gather(shard, axis)  36.5 us
    dot_general x32, matrix products, one_row(): jnp.dot(factor_row, inverse, precision=lax.Precision.HIGHEST)  24.9 us
    add x3, other arithmetic, per_device(): field_now = field_now + 0.5 * time_step * (slope_one + slope_two)  23.8 us
    add x3, other arithmetic, per_device(): middle = field_now + time_step * slope_one  20.3 us
    reduce_sum x32, other arithmetic, one_row(): pivot = jnp.sum(factor_row * unit_row)  19.5 us
  transfers between devices with their start and end apart: 27, of which 13 were waited for; matrix products, arithmetic and copies ran while one was open for 13% of the time, Pallas kernels for 0%

profile of v1, /device:TPU:0, one launch (start us, length us, event | category | flops | bytes accessed | tf_op | source)
XLA Modules:
  0.0 409.8 jit_solution(13626814360584305634)
XLA Ops:
  2.8 4.6 %collective-permute-start.1 = (f32[32,5,2,128]{3,0,2,1:T(8,128)}, f32[32,5,2,128]{3,0,2,1:T(8,128)}, u32[]{:S(2)}, u32[]{:S(2)}) collective-permute-start(f32[32,5,2,128]{3,0,2,1:T(8,128)} %copy.298), channel_id=1, source_target_pairs={{0,8},{8,16},{16,24},{24,32},{32,40},{40,48},{48,56},{56,64},{64,7... | collective-permute-start | bytes 491528 | tf_op jit(solution)/shard_map/ppermute | solution.py:26
  9.4 4.3 %copy.227 = f32[32,5,16,128]{0,2,3,1:T(8,128)} copy(f32[32,5,16,128]{3,2,1,0:T(8,128)S(1)} %copy-done) | data formatting | bytes 2621440 | tf_op args[0]
  19.7 3.5 pad_maximum_fusion
  23.2 3.1 copy-done.1
  27.7 3.0 collective-permute-start.3
  36.0 6.5 %copy.229 = f32[32,5,20,128]{3,0,2,1:T(8,128)} copy(f32[32,5,20,128]{0,2,3,1:T(8,128)} %copy-done.1) | data formatting | bytes 3276800 | tf_op jit(solution)/shard_map/concatenate | solution.py:28
  46.2 8.7 %multiply_add_fusion.7 = (f32[32,5,16,128]{3,0,2,1:T(8,128)S(1)}, f32[32,5,16,128]{3,0,2,1:T(8,128)}) fusion(f32[32,5,16,128]{3,2,1,0:T(8,128)S(1)} %copy-done, f32[32,16,128]{2,0,1:T(8,128)} %copy.238, f32[5,16,128]{2,1,0:T(8,128)S(1)} %get-tuple-element.336, f32[32,16,128]{2,0,1:T(8,128)} %copy.237, f32[5,16,128]{2,1,0:T(8,128)S(1)} %get-tuple-element.337, ...), kind=kLoop, calls=%fused_computation.117 | loop fusion | flops 12779520 | bytes 12396564 | tf_op jit(solution)/shard_map/add | solution.py:98
  56.2 5.2 %collective-permute-start.5 = (f32[32,5,2,128]{3,0,2,1:T(8,128)S(1)}, f32[32,5,2,128]{3,0,2,1:T(8,128)S(1)}, u32[]{:S(2)}, u32[]{:S(2)}) collective-permute-start(f32[32,5,2,128]{3,0,2,1:T(8,128)S(1)} %get-tuple-element.322), channel_id=1, source_target_pairs={{0,8},{8,16},{16,24},{24,32},{32,40},{40,48},{48,56},{56,64},{64,7... | collective-permute-start | bytes 491528 | tf_op jit(solution)/shard_map/ppermute | solution.py:26
  61.4 2.7 collective-permute-done.4
  66.4 2.2 fusion.27
  72.2 2.9 copy.278
  75.0 3.7 collective-permute-start.7
  79.6 2.8 copy.241
  82.4 2.7 copy.243
  85.1 9.4 %multiply_add_fusion.6 = f32[32,5,16,128]{3,0,2,1:T(8,128)S(1)} fusion(f32[32,5,16,128]{3,0,2,1:T(8,128)} %get-tuple-element.276, f32[32,5,16,128]{3,0,2,1:T(8,128)} %copy-done.2, f32[32,5,20,2]{3,0,2,1:T(8,128)} %copy.241, f32[32,5,2,128]{3,0,2,1:T(8,128)} %copy-done.8, f32[32,5,2,128]{3,0,2,1:T(8,128)} %copy-done.12, f32[32,5,20,2]{3,0,2,1:T(8,128)} %copy.243, ...), kind=kLoop, calls=%fused_computation.116 | loop fusion | flops 17039360 | bytes 7153684 | tf_op jit(solution)/shard_map/add | solution.py:100
  95.8 5.2 %collective-permute-start.9 = (f32[32,5,2,128]{3,0,2,1:T(8,128)S(1)}, f32[32,5,2,128]{3,0,2,1:T(8,128)S(1)}, u32[]{:S(2)}, u32[]{:S(2)}) collective-permute-start(f32[32,5,2,128]{3,0,2,1:T(8,128)S(1)} %get-tuple-element.310), channel_id=1, source_target_pairs={{0,8},{8,16},{16,24},{24,32},{32,40},{40,48},{48,56},{56,64},{64,7... | collective-permute-start | bytes 491528 | tf_op jit(solution)/shard_map/ppermute | solution.py:26
  101.1 2.9 collective-permute-done.8
  105.8 2.3 fusion.26
  108.1 2.2 copy.279
  111.6 2.2 copy.280
  113.8 3.0 collective-permute-start.11
  121.5 5.8 %multiply_add_fusion.4 = (f32[32,5,16,128]{3,0,2,1:T(8,128)S(1)}, f32[32,5,16,128]{3,0,2,1:T(8,128)}) fusion(f32[32,5,16,128]{3,0,2,1:T(8,128)S(1)} %multiply_add_fusion.6, f32[32,16,128]{2,0,1:T(8,128)} %get-tuple-element.316, f32[5,16,128]{2,1,0:T(8,128)S(1)} %get-tuple-element.336, f32[32,16,128]{2,0,1:T(8,128)S(1)} %get-tuple-element.313, ...), kind=kLoop, calls=%fused_computation.114 | loop fusion | flops 16711680 | bytes 5842964 | tf_op jit(solution)/shard_map/add | solution.py:98
  128.6 5.0 %collective-permute-start.13 = (f32[32,5,2,128]{3,0,2,1:T(8,128)S(1)}, f32[32,5,2,128]{3,0,2,1:T(8,128)S(1)}, u32[]{:S(2)}, u32[]{:S(2)}) collective-permute-start(f32[32,5,2,128]{3,0,2,1:T(8,128)S(1)} %get-tuple-element.308), channel_id=1, source_target_pairs={{0,8},{8,16},{16,24},{24,32},{32,40},{40,48},{48,56},{56,64},{64,7... | collective-permute-start | bytes 491528 | tf_op jit(solution)/shard_map/ppermute | solution.py:26
  133.7 2.7 collective-permute-done.12
  138.7 2.2 fusion.25
  140.9 2.2 copy.281
  144.4 2.9 copy.282
  147.3 3.7 collective-permute-start.15
  151.8 2.8 copy.250
  154.6 2.7 copy.252
  157.3 9.3 %multiply_add_fusion.3 = f32[32,5,16,128]{3,0,2,1:T(8,128)S(1)} fusion(f32[32,5,16,128]{3,0,2,1:T(8,128)S(1)} %multiply_add_fusion.6, f32[32,5,16,128]{3,0,2,1:T(8,128)} %get-tuple-element.274, f32[32,5,16,128]{3,0,2,1:T(8,128)} %copy-done.3, f32[32,5,20,2]{3,0,2,1:T(8,128)} %copy.250, f32[32,5,2,128]{3,0,2,1:T(8,128)} %copy-done.7, ...), kind=kLoop, calls=%fused_computation.113 | loop fusion | flops 17039360 | bytes 7153684 | tf_op jit(solution)/shard_map/add | solution.py:100
  168.0 5.0 %collective-permute-start.17 = (f32[32,5,2,128]{3,0,2,1:T(8,128)S(1)}, f32[32,5,2,128]{3,0,2,1:T(8,128)S(1)}, u32[]{:S(2)}, u32[]{:S(2)}) collective-permute-start(f32[32,5,2,128]{3,0,2,1:T(8,128)S(1)} %get-tuple-element.296), channel_id=1, source_target_pairs={{0,8},{8,16},{16,24},{24,32},{32,40},{40,48},{48,56},{56,64},{64,7... | collective-permute-start | bytes 491528 | tf_op jit(solution)/shard_map/ppermute | solution.py:26
  173.0 2.8 collective-permute-done.16
  185.0 3.2 collective-permute-start.19
  189.2 2.8 copy.254
  193.8 5.8 %multiply_add_fusion.1 = (f32[32,5,16,128]{3,0,2,1:T(8,128)S(1)}, f32[32,5,16,128]{3,0,2,1:T(8,128)}) fusion(f32[32,5,16,128]{3,0,2,1:T(8,128)S(1)} %multiply_add_fusion.3, f32[32,16,128]{2,0,1:T(8,128)} %get-tuple-element.302, f32[5,16,128]{2,1,0:T(8,128)S(1)} %get-tuple-element.336, f32[32,16,128]{2,0,1:T(8,128)S(1)} %get-tuple-element.299, ...), kind=kLoop, calls=%fused_computation.111 | loop fusion | flops 16711680 | bytes 5842964 | tf_op jit(solution)/shard_map/add | solution.py:98
  200.9 6.9 %collective-permute-start.21 = (f32[32,5,2,128]{3,0,2,1:T(8,128)S(1)}, f32[32,5,2,128]{3,0,2,1:T(8,128)S(1)}, u32[]{:S(2)}, u32[]{:S(2)}) collective-permute-start(f32[32,5,2,128]{3,0,2,1:T(8,128)S(1)} %get-tuple-element.294), channel_id=1, source_target_pairs={{0,8},{8,16},{16,24},{24,32},{32,40},{40,48},{48,56},{56,64},{64,7... | collective-permute-start | bytes 491528 | tf_op jit(solution)/shard_map/ppermute | solution.py:26
  207.8 2.4 collective-permute-done.20
  212.6 2.2 fusion.23
  218.3 2.9 copy.286
  221.2 3.7 collective-permute-start.23
  225.8 2.8 copy.258
  228.6 2.7 copy.260
  231.3 5.1 %multiply_add_fusion = f32[32,5,16,128]{3,0,2,1:T(8,128)S(1)} fusion(f32[32,5,16,128]{3,0,2,1:T(8,128)S(1)} %multiply_add_fusion.3, f32[32,5,16,128]{3,0,2,1:T(8,128)} %get-tuple-element.272, f32[32,5,16,128]{3,0,2,1:T(8,128)S(1)} %get-tuple-element.271, f32[32,5,20,2]{3,0,2,1:T(8,128)} %copy.258, f32[32,5,2,128]{3,0,2,1:T(8,128)} %copy-done.5, ...), kind=kLoop, calls=%fused_computation.110 | loop fusion | flops 17039360 | bytes 7153684 | tf_op jit(solution)/shard_map/add | solution.py:100
  240.8 2.6 collective-permute-done.25
  248.7 2.9 cholesky.55
  253.0 36.5 %all-gather = f32[512,32]{1,0:T(8,128)S(1)} all-gather(f32[32,32]{1,0:T(8,128)S(1)} %copy.263), channel_id=2, replica_groups=mesh['ax'=16,'rad'=8] {'ax'}, dimensions={0}, use_global_device_ids=true | all-gather | bytes 69632 | tf_op jit(solution)/shard_map/all_gather | solution.py:33
  289.6 70.9 %while.30 = (s32[]{:T(128)}, f32[32,32]{0,1:T(8,128)S(1)}, f32[16,32,32]{2,1,0:T(8,128)S(1)}, s32[]{:T(128)}, s32[]{:T(128)}, /*index=5*/s32[]{:T(128)}) while((s32[]{:T(128)}, f32[32,32]{0,1:T(8,128)S(1)}, f32[16,32,32]{2,1,0:T(8,128)S(1)}, s32[]{:T(128)}, s32[]{:T(128)}, /*index=5*/s32[]{:T(128)}) %tuple.141), condition=%wide.region_3.5_spmd, body=%wide.region_2.4_spmd.sunk | while | flops 795684 | bytes 78197 | solution.py:39
  290.1 2.9 cholesky.109
  294.8 2.9 cholesky.109
  299.5 2.9 cholesky.109
  304.3 2.9 cholesky.109
  309.0 2.9 cholesky.109
  313.7 2.9 cholesky.109
  318.5 2.9 cholesky.109
  323.2 2.9 cholesky.109
  327.9 2.9 cholesky.109
  332.6 2.9 cholesky.109
  337.4 2.9 cholesky.109
  342.1 2.9 cholesky.109
  346.8 2.9 cholesky.109
  351.6 2.9 cholesky.109
  356.3 2.9 cholesky.109
  360.6 45.8 %while.31 = (s32[]{:T(128)}, f32[32,32]{1,0:T(8,128)S(1)}, f32[32,32]{1,0:T(8,128)S(1)}, f32[32,32]{1,0:T(8,128)S(1)}, s32[]{:T(128)}, /*index=5*/s32[]{:T(128)}, s32[]{:T(128)}, s32[]{:T(128)}) while((s32[]{:T(128)}, f32[32,32]{1,0:T(8,128)S(1)}, f32[32,32]{1,0:T(8,128)S(1)}, f32[32,32]{1,0:T(8,128)S(1)}, s32[]{:T(128)}, ...), condition=%wide.region_6.8_spmd, body=%wide.region_4.7_spmd.sunk | while | flops 12421 | bytes 19219 | solution.py:79
  (349 shorter events, 150.9 us)
Async XLA Ops:
  0.6 8.7 %copy-start = (f32[32,5,16,128]{3,2,1,0:T(8,128)S(1)}, f32[32,5,16,128]{3,2,1,0:T(8,128)}, u32[]{:S(2)}) copy-start(f32[32,5,16,128]{3,2,1,0:T(8,128)} %param.10) | copy-start | bytes 3932164
  2.8 14.4 %collective-permute-start.1 = (f32[32,5,2,128]{3,0,2,1:T(8,128)}, f32[32,5,2,128]{3,0,2,1:T(8,128)}, u32[]{:S(2)}, u32[]{:S(2)}) collective-permute-start(f32[32,5,2,128]{3,0,2,1:T(8,128)} %copy.298), channel_id=1, source_target_pairs={{0,8},{8,16},{16,24},{24,32},{32,40},{40,48},{48,56},{56,64},{64,7... | collective-permute-start | bytes 491528 | tf_op jit(solution)/shard_map/ppermute | solution.py:26
  8.1 10.4 %collective-permute-start = (f32[32,5,2,128]{3,0,2,1:T(8,128)}, f32[32,5,2,128]{3,0,2,1:T(8,128)}, u32[]{:S(2)}, u32[]{:S(2)}) collective-permute-start(f32[32,5,2,128]{3,0,2,1:T(8,128)} %copy.297), channel_id=1, source_target_pairs={{8,0},{16,8},{24,16},{32,24},{40,32},{48,40},{56,48},{64,56},{72,6... | collective-permute-start | bytes 491528 | tf_op jit(solution)/shard_map/ppermute | solution.py:27
  13.7 0.9 copy-start.15
  14.6 2.6 copy-start.22
  14.6 2.6 copy-start.23
  14.7 2.6 copy-start.24
  17.2 28.9 %copy-start.17 = (f32[5]{0:T(128)}, f32[5]{0:T(128)S(1)}, u32[]{:S(2)}) copy-start(f32[5]{0:T(128)S(1)} %broadcast_multiply_fusion.1) | copy-start | bytes 64
  23.2 3.1 copy-start.1
  26.4 16.1 %collective-permute-start.2 = (f32[32,5,20,2]{0,2,3,1:T(8,128)S(1)}, f32[32,5,20,2]{0,2,3,1:T(8,128)S(1)}, u32[]{:S(2)}, u32[]{:S(2)}) collective-permute-start(f32[32,5,20,2]{0,2,3,1:T(8,128)S(1)} %get-tuple-element.277), channel_id=1, source_target_pairs={{1,0},{2,1},{3,2},{4,3},{5,4},{6,5},{7,6},{9,8},{10,9},{11,10},{12... | collective-permute-start | bytes 76808 | tf_op jit(solution)/shard_map/ppermute | solution.py:27
  27.7 16.6 %collective-permute-start.3 = (f32[32,5,20,2]{0,2,3,1:T(8,128)S(1)}, f32[32,5,20,2]{0,2,3,1:T(8,128)S(1)}, u32[]{:S(2)}, u32[]{:S(2)}) collective-permute-start(f32[32,5,20,2]{0,2,3,1:T(8,128)S(1)} %get-tuple-element.278), channel_id=1, source_target_pairs={{0,1},{1,2},{2,3},{3,4},{4,5},{5,6},{6,7},{8,9},{9,10},{10,11},{11... | collective-permute-start | bytes 76808 | tf_op jit(solution)/shard_map/ppermute | solution.py:26
  54.9 23.8 %copy-start.2 = (f32[32,5,16,128]{3,0,2,1:T(8,128)}, f32[32,5,16,128]{3,0,2,1:T(8,128)S(1)}, u32[]{:S(2)}) copy-start(f32[32,5,16,128]{3,0,2,1:T(8,128)S(1)} %get-tuple-element.275) | copy-start | bytes 3932164
  54.9 9.2 %collective-permute-start.4 = (f32[32,5,2,128]{3,0,2,1:T(8,128)S(1)}, f32[32,5,2,128]{3,0,2,1:T(8,128)S(1)}, u32[]{:S(2)}, u32[]{:S(2)}) collective-permute-start(f32[32,5,2,128]{3,0,2,1:T(8,128)S(1)} %get-tuple-element.323), channel_id=1, source_target_pairs={{8,0},{16,8},{24,16},{32,24},{40,32},{48,40},{56,48},{64,56},{72,6... | collective-permute-start | bytes 491528 | tf_op jit(solution)/shard_map/ppermute | solution.py:27
  56.2 9.5 %collective-permute-start.5 = (f32[32,5,2,128]{3,0,2,1:T(8,128)S(1)}, f32[32,5,2,128]{3,0,2,1:T(8,128)S(1)}, u32[]{:S(2)}, u32[]{:S(2)}) collective-permute-start(f32[32,5,2,128]{3,0,2,1:T(8,128)S(1)} %get-tuple-element.322), channel_id=1, source_target_pairs={{0,8},{8,16},{16,24},{24,32},{32,40},{40,48},{48,56},{56,64},{64,7... | collective-permute-start | bytes 491528 | tf_op jit(solution)/shard_map/ppermute | solution.py:26
  64.1 1.8 copy-start.8
  65.8 0.7 copy-start.12
  70.9 8.7 %collective-permute-start.6 = (f32[32,5,20,2]{0,2,3,1:T(8,128)S(1)}, f32[32,5,20,2]{0,2,3,1:T(8,128)}, u32[]{:S(2)}, u32[]{:S(2)}) collective-permute-start(f32[32,5,20,2]{0,2,3,1:T(8,128)S(1)} %copy.277), channel_id=1, source_target_pairs={{1,0},{2,1},{3,2},{4,3},{5,4},{6,5},{7,6},{9,8},{10,9},{11,10},{12... | collective-permute-start | bytes 76808 | tf_op jit(solution)/shard_map/ppermute | solution.py:27
  75.0 7.4 %collective-permute-start.7 = (f32[32,5,20,2]{0,2,3,1:T(8,128)}, f32[32,5,20,2]{0,2,3,1:T(8,128)}, u32[]{:S(2)}, u32[]{:S(2)}) collective-permute-start(f32[32,5,20,2]{0,2,3,1:T(8,128)} %copy.278), channel_id=1, source_target_pairs={{0,1},{1,2},{2,3},{3,4},{4,5},{5,6},{6,7},{8,9},{9,10},{10,11},{11... | collective-permute-start | bytes 76808 | tf_op jit(solution)/shard_map/ppermute | solution.py:26
  82.4 2.7 copy-start.18
  94.5 9.4 %collective-permute-start.8 = (f32[32,5,2,128]{3,0,2,1:T(8,128)S(1)}, f32[32,5,2,128]{3,0,2,1:T(8,128)S(1)}, u32[]{:S(2)}, u32[]{:S(2)}) collective-permute-start(f32[32,5,2,128]{3,0,2,1:T(8,128)S(1)} %get-tuple-element.311), channel_id=1, source_target_pairs={{8,0},{16,8},{24,16},{32,24},{40,32},{48,40},{56,48},{64,56},{72,6... | collective-permute-start | bytes 491528 | tf_op jit(solution)/shard_map/ppermute | solution.py:27
  95.8 9.4 %collective-permute-start.9 = (f32[32,5,2,128]{3,0,2,1:T(8,128)S(1)}, f32[32,5,2,128]{3,0,2,1:T(8,128)S(1)}, u32[]{:S(2)}, u32[]{:S(2)}) collective-permute-start(f32[32,5,2,128]{3,0,2,1:T(8,128)S(1)} %get-tuple-element.310), channel_id=1, source_target_pairs={{0,8},{8,16},{16,24},{24,32},{32,40},{40,48},{48,56},{56,64},{64,7... | collective-permute-start | bytes 491528 | tf_op jit(solution)/shard_map/ppermute | solution.py:26
  103.9 1.4 copy-start.9
  105.2 0.7 copy-start.13
  110.3 7.5 %collective-permute-start.10 = (f32[32,5,20,2]{0,2,3,1:T(8,128)S(1)}, f32[32,5,20,2]{0,2,3,1:T(8,128)S(1)}, u32[]{:S(2)}, u32[]{:S(2)}) collective-permute-start(f32[32,5,20,2]{0,2,3,1:T(8,128)S(1)} %copy.279), channel_id=1, source_target_pairs={{1,0},{2,1},{3,2},{4,3},{5,4},{6,5},{7,6},{9,8},{10,9},{11,10},{12... | collective-permute-start | bytes 76808 | tf_op jit(solution)/shard_map/ppermute | solution.py:27
  113.8 5.8 %collective-permute-start.11 = (f32[32,5,20,2]{0,2,3,1:T(8,128)S(1)}, f32[32,5,20,2]{0,2,3,1:T(8,128)S(1)}, u32[]{:S(2)}, u32[]{:S(2)}) collective-permute-start(f32[32,5,20,2]{0,2,3,1:T(8,128)S(1)} %copy.280), channel_id=1, source_target_pairs={{0,1},{1,2},{2,3},{3,4},{4,5},{5,6},{6,7},{8,9},{9,10},{10,11},{11... | collective-permute-start | bytes 76808 | tf_op jit(solution)/shard_map/ppermute | solution.py:26
  127.3 23.6 %copy-start.3 = (f32[32,5,16,128]{3,0,2,1:T(8,128)}, f32[32,5,16,128]{3,0,2,1:T(8,128)S(1)}, u32[]{:S(2)}) copy-start(f32[32,5,16,128]{3,0,2,1:T(8,128)S(1)} %get-tuple-element.273) | copy-start | bytes 3932164
  127.3 9.0 %collective-permute-start.12 = (f32[32,5,2,128]{3,0,2,1:T(8,128)S(1)}, f32[32,5,2,128]{3,0,2,1:T(8,128)S(1)}, u32[]{:S(2)}, u32[]{:S(2)}) collective-permute-start(f32[32,5,2,128]{3,0,2,1:T(8,128)S(1)} %get-tuple-element.309), channel_id=1, source_target_pairs={{8,0},{16,8},{24,16},{32,24},{40,32},{48,40},{56,48},{64,56},{72,6... | collective-permute-start | bytes 491528 | tf_op jit(solution)/shard_map/ppermute | solution.py:27
  128.6 9.4 %collective-permute-start.13 = (f32[32,5,2,128]{3,0,2,1:T(8,128)S(1)}, f32[32,5,2,128]{3,0,2,1:T(8,128)S(1)}, u32[]{:S(2)}, u32[]{:S(2)}) collective-permute-start(f32[32,5,2,128]{3,0,2,1:T(8,128)S(1)} %get-tuple-element.308), channel_id=1, source_target_pairs={{0,8},{8,16},{16,24},{24,32},{32,40},{40,48},{48,56},{56,64},{64,7... | collective-permute-start | bytes 491528 | tf_op jit(solution)/shard_map/ppermute | solution.py:26
  136.3 1.8 copy-start.7
  138.0 0.7 copy-start.11
  143.1 8.7 %collective-permute-start.14 = (f32[32,5,20,2]{0,2,3,1:T(8,128)S(1)}, f32[32,5,20,2]{0,2,3,1:T(8,128)}, u32[]{:S(2)}, u32[]{:S(2)}) collective-permute-start(f32[32,5,20,2]{0,2,3,1:T(8,128)S(1)} %copy.281), channel_id=1, source_target_pairs={{1,0},{2,1},{3,2},{4,3},{5,4},{6,5},{7,6},{9,8},{10,9},{11,10},{12... | collective-permute-start | bytes 76808 | tf_op jit(solution)/shard_map/ppermute | solution.py:27
  147.3 7.4 %collective-permute-start.15 = (f32[32,5,20,2]{0,2,3,1:T(8,128)}, f32[32,5,20,2]{0,2,3,1:T(8,128)}, u32[]{:S(2)}, u32[]{:S(2)}) collective-permute-start(f32[32,5,20,2]{0,2,3,1:T(8,128)} %copy.282), channel_id=1, source_target_pairs={{0,1},{1,2},{2,3},{3,4},{4,5},{5,6},{6,7},{8,9},{9,10},{10,11},{11... | collective-permute-start | bytes 76808 | tf_op jit(solution)/shard_map/ppermute | solution.py:26
  154.6 2.7 copy-start.19
  166.7 9.1 %collective-permute-start.16 = (f32[32,5,2,128]{3,0,2,1:T(8,128)S(1)}, f32[32,5,2,128]{3,0,2,1:T(8,128)S(1)}, u32[]{:S(2)}, u32[]{:S(2)}) collective-permute-start(f32[32,5,2,128]{3,0,2,1:T(8,128)S(1)} %get-tuple-element.297), channel_id=1, source_target_pairs={{8,0},{16,8},{24,16},{32,24},{40,32},{48,40},{56,48},{64,56},{72,6... | collective-permute-start | bytes 491528 | tf_op jit(solution)/shard_map/ppermute | solution.py:27
  168.0 9.5 %collective-permute-start.17 = (f32[32,5,2,128]{3,0,2,1:T(8,128)S(1)}, f32[32,5,2,128]{3,0,2,1:T(8,128)S(1)}, u32[]{:S(2)}, u32[]{:S(2)}) collective-permute-start(f32[32,5,2,128]{3,0,2,1:T(8,128)S(1)} %get-tuple-element.296), channel_id=1, source_target_pairs={{0,8},{8,16},{16,24},{24,32},{32,40},{40,48},{48,56},{56,64},{64,7... | collective-permute-start | bytes 491528 | tf_op jit(solution)/shard_map/ppermute | solution.py:26
  175.8 1.7 copy-start.10
  177.5 0.7 copy-start.14
  182.2 6.9 %collective-permute-start.18 = (f32[32,5,20,2]{0,2,3,1:T(8,128)S(1)}, f32[32,5,20,2]{0,2,3,1:T(8,128)}, u32[]{:S(2)}, u32[]{:S(2)}) collective-permute-start(f32[32,5,20,2]{0,2,3,1:T(8,128)S(1)} %copy.283), channel_id=1, source_target_pairs={{1,0},{2,1},{3,2},{4,3},{5,4},{6,5},{7,6},{9,8},{10,9},{11,10},{12... | collective-permute-start | bytes 76808 | tf_op jit(solution)/shard_map/ppermute | solution.py:27
  185.0 7.0 %collective-permute-start.19 = (f32[32,5,20,2]{0,2,3,1:T(8,128)}, f32[32,5,20,2]{0,2,3,1:T(8,128)S(1)}, u32[]{:S(2)}, u32[]{:S(2)}) collective-permute-start(f32[32,5,20,2]{0,2,3,1:T(8,128)} %copy.284), channel_id=1, source_target_pairs={{0,1},{1,2},{2,3},{3,4},{4,5},{5,6},{6,7},{8,9},{9,10},{10,11},{11... | collective-permute-start | bytes 76808 | tf_op jit(solution)/shard_map/ppermute | solution.py:26
  191.9 1.8 copy-start.20
  199.6 10.6 %collective-permute-start.20 = (f32[32,5,2,128]{3,0,2,1:T(8,128)S(1)}, f32[32,5,2,128]{3,0,2,1:T(8,128)S(1)}, u32[]{:S(2)}, u32[]{:S(2)}) collective-permute-start(f32[32,5,2,128]{3,0,2,1:T(8,128)S(1)} %get-tuple-element.295), channel_id=1, source_target_pairs={{8,0},{16,8},{24,16},{32,24},{40,32},{48,40},{56,48},{64,56},{72,6... | collective-permute-start | bytes 491528 | tf_op jit(solution)/shard_map/ppermute | solution.py:27
  200.9 11.1 %collective-permute-start.21 = (f32[32,5,2,128]{3,0,2,1:T(8,128)S(1)}, f32[32,5,2,128]{3,0,2,1:T(8,128)S(1)}, u32[]{:S(2)}, u32[]{:S(2)}) collective-permute-start(f32[32,5,2,128]{3,0,2,1:T(8,128)S(1)} %get-tuple-element.294), channel_id=1, source_target_pairs={{0,8},{8,16},{16,24},{24,32},{32,40},{40,48},{48,56},{56,64},{64,7... | collective-permute-start | bytes 491528 | tf_op jit(solution)/shard_map/ppermute | solution.py:26
  210.2 1.9 copy-start.5
  211.9 0.7 copy-start.6
  217.0 8.8 %collective-permute-start.22 = (f32[32,5,20,2]{0,2,3,1:T(8,128)S(1)}, f32[32,5,20,2]{0,2,3,1:T(8,128)}, u32[]{:S(2)}, u32[]{:S(2)}) collective-permute-start(f32[32,5,20,2]{0,2,3,1:T(8,128)S(1)} %copy.285), channel_id=1, source_target_pairs={{1,0},{2,1},{3,2},{4,3},{5,4},{6,5},{7,6},{9,8},{10,9},{11,10},{12... | collective-permute-start | bytes 76808 | tf_op jit(solution)/shard_map/ppermute | solution.py:27
  221.2 7.4 %collective-permute-start.23 = (f32[32,5,20,2]{0,2,3,1:T(8,128)}, f32[32,5,20,2]{0,2,3,1:T(8,128)}, u32[]{:S(2)}, u32[]{:S(2)}) collective-permute-start(f32[32,5,20,2]{0,2,3,1:T(8,128)} %copy.286), channel_id=1, source_target_pairs={{0,1},{1,2},{2,3},{3,4},{4,5},{5,6},{6,7},{8,9},{9,10},{10,11},{11... | collective-permute-start | bytes 76808 | tf_op jit(solution)/shard_map/ppermute | solution.py:26
  228.6 2.7 copy-start.21
  236.4 1.2 copy-start.4
  237.6 2.0 collective-permute-start.24
  239.6 3.7 collective-permute-start.25
  243.4 5.2 %collective-permute-start.26 = (f32[32,32]{0,1:T(8,128)S(1)}, f32[32,32]{0,1:T(8,128)S(1)}, u32[]{:S(2)}, u32[]{:S(2)}) collective-permute-start(f32[32,32]{0,1:T(8,128)S(1)} %add.416), channel_id=1, source_target_pairs={{0,4},{1,5},{2,6},{3,7},{4,0},{5,1},{6,2},{7,3},{8,12},{9,13},{10,... | collective-permute-start | bytes 12296 | tf_op jit(solution)/shard_map/ppermute | solution.py:14
  406.5 1.5 copy-start.16
